TPU v7x, 32 devices: a whole 2x2x4 slice. The times are simulated.
32 devices in a mesh: row: 4 (over y, x), col: 8 (over z, core).
Axes of the slice: x: 2, y: 2, z: 4, core: 2. Of those that a mesh axis runs over, the one named last changes fastest.
Arguments:
- sim: bfloat16 [8192, 8192], P('row', 'col'), may hold values from -6 to 6
- diag_blocks: bfloat16 [2048, 8192], P(None, 'col'), may hold values from -0.125 to 0.125
- match_perm: int32 [4, 2048], replicated, may hold values from 0 to 2047, each once within a row
- match_scale: float32 [4, 2048], replicated, may hold values from 0.3 to 1.5
- features: bfloat16 [8192, 256], P('col'), may hold values from -0.0625 to 0.0625
Outputs:
- new_sim: bfloat16 [8192, 8192], P('row', 'col')
- aggregated: float32 [8192, 256], P(('row', 'col'))
Inputs may be any that keep to these rules, and one draw needn't show every extreme that they name: Each row of match_perm lists every number of 0 to 2047 once.
All inputs are finite; a program needn't handle non-finite values.
Results may differ from a plain program's by a relative error of at most 0.0058.
Values may be sent and summed in bfloat16 or wider, within the bound.
No kernel may reach another device: no remote copies, remote signals or barrier semaphores. Data moves between devices by JAX's collectives and lax.ppermute only.
A program may use at most 128 MiB of HBM per device.

v0:
```python
import jax
import jax.numpy as jnp
from jax import lax
from jax.sharding import PartitionSpec as P

decay_factor = 0.8


def partner_2(value, axis, bit):
    mask = 2**bit
    pairs = [(source, source ^ mask) for source in range(lax.axis_size(axis))]
    return lax.ppermute(value, axis, pairs)


def shifted(value, axis, steps):
    count = lax.axis_size(axis)
    pairs = [(source, (source + steps) % count) for source in range(count)]
    return lax.ppermute(value, axis, pairs)


def spread(x, axis, root):
    mine = lax.axis_index(axis) == root
    return lax.psum(jnp.where(mine, x, jnp.zeros_like(x)), axis)


def on_device(sim, diag_blocks, match_perm, match_scale, features):
    row_count = lax.axis_size("row")
    col_count = lax.axis_size("col")
    blocks_here = col_count // 2 // row_count
    row_id = lax.axis_index("row")
    col_id = lax.axis_index("col")
    block_id = col_id // 2
    side = col_id % 2
    half_width = sim.shape[1]
    tile_rows = sim.shape[0]
    partner = partner_2(sim, "col", 0)
    first_half = jnp.where(side == 0, sim, partner)
    second_half = jnp.where(side == 0, partner, sim)
    whole_block = jnp.concatenate([first_half, second_half], axis=1)
    perm_block = lax.dynamic_index_in_dim(match_perm, block_id, 0, keepdims=False)
    scale_block = lax.dynamic_index_in_dim(match_scale, block_id, 0, keepdims=False)
    own_perm = lax.dynamic_slice_in_dim(perm_block, side * half_width, half_width, 0)
    own_scale = lax.dynamic_slice_in_dim(scale_block, side * half_width, half_width, 0)
    moved_cols = (jnp.take(whole_block, own_perm, axis=1) * own_scale[None, :]).astype(jnp.bfloat16)
    arrived_cols = shifted(moved_cols, "col", col_count // 2)
    mixed = (
        jnp.dot(whole_block, diag_blocks, preferred_element_type=jnp.float32) + arrived_cols
    ).astype(jnp.bfloat16)
    position = 0
    source = row_id * blocks_here + position
    perm_rows = lax.dynamic_index_in_dim(match_perm, source, 0, keepdims=False)
    scale_rows = lax.dynamic_index_in_dim(match_scale, source, 0, keepdims=False)
    sent_rows = (jnp.take(mixed, perm_rows, axis=0) * scale_rows[:, None]).astype(jnp.bfloat16)
    arrived_rows = shifted(sent_rows, "row", row_count // 2)
    position = 0
    target = row_id * blocks_here + position
    halves = []
    for part in range(2):
        left_half = spread(diag_blocks, "col", 2 * target + part)
        halves.append(
            lax.dot_general(
                left_half, mixed, (((0,), (0,)), ((), ())), preferred_element_type=jnp.float32
            )
        )
    product = jnp.concatenate(halves, axis=0)
    results = decay_factor * (product + arrived_rows)
    global_rows = row_id * tile_rows + lax.broadcasted_iota(jnp.int32, results.shape, 0)
    global_cols = col_id * half_width + lax.broadcasted_iota(jnp.int32, results.shape, 1)
    new_sim = jnp.where(global_rows == global_cols, 1.0, results).astype(jnp.bfloat16)
    partial_value = jnp.dot(new_sim, features, preferred_element_type=jnp.float32)
    aggregated = lax.psum_scatter(partial_value, "col", scatter_dimension=0, tiled=True)
    return (new_sim, aggregated)


def solution(mesh):
    placed = (P("row", "col"), P(None, "col"), P(), P(), P("col", None))
    return jax.shard_map(
        on_device,
        mesh=mesh,
        in_specs=placed,
        out_specs=(P("row", "col"), P(("row", "col"), None)),
        check_vma=False,
    )
```

profile of v0, /device:TPU:0, one launch (start us, length us, event | category | flops | bytes accessed | tf_op | source)
XLA Modules:
  0.0 503.9 jit_solution(8184790162820065224)
XLA Ops:
  7.2 6.5 %copy.12 = bf16[2048,1024]{0,1:T(8,128)(2,1)} copy(bf16[2048,1024]{1,0:T(8,128)(2,1)} %param.5) | data formatting | bytes 8388608 | tf_op args[0]
  14.2 0.8 dynamic_slice.23
  15.0 0.8 compare_select_fusion.1
  15.8 5.5 %collective-permute-done = bf16[2048,1024]{0,1:T(8,128)(2,1)} collective-permute-done((bf16[2048,1024]{0,1:T(8,128)(2,1)}, bf16[2048,1024]{0,1:T(8,128)(2,1)}, u32[]{:S(2)}, u32[]{:S(2)}) %collective-permute-start) | collective-permute-done | bytes 4194336 | tf_op jit(solution)/shard_map/ppermute | solution.py:12
  21.3 5.7 %broadcast_select_fusion.2 = (bf16[2048,1024]{0,1:T(8,128)(2,1)}, bf16[2048,1024]{0,1:T(8,128)(2,1)}) fusion(bf16[2048,1024]{0,1:T(8,128)(2,1)} %copy.12, bf16[2048,1024]{0,1:T(8,128)(2,1)} %collective-permute-done, pred[]{:T(512)S(6)} %eq.17), kind=kLoop, calls=%fused_computation.13 | loop fusion | flops 4194304 | bytes 16777216 | tf_op jit(solution)/shard_map/jit(_where)/select_n | solution.py:37
  27.0 8.4 %pad_maximum_fusion = bf16[2048,2048]{0,1:T(8,128)(2,1)} fusion(bf16[2048,1024]{0,1:T(8,128)(2,1)} %get-tuple-element.9, bf16[2048,1024]{0,1:T(8,128)(2,1)} %get-tuple-element.8), kind=kLoop, calls=%fused_computation.2 | loop fusion | flops 16777216 | bytes 16777216 | tf_op jit(solution)/shard_map/concatenate | solution.py:39
  35.4 13.3 %gather_fusion = bf16[1024,2048]{1,0:T(8,128)(2,1)} fusion(bf16[2048,2048]{0,1:T(8,128)(2,1)} %pad_maximum_fusion, s32[1024]{0:T(1024)S(1)} %broadcast_clamp_fusion.1), kind=kCustom, calls=%fused_computation | custom fusion | bytes 8392704 | tf_op jit(solution)/shard_map/jit(_take)/gather | solution.py:44
  48.7 6.4 %copy.14 = bf16[1024,2048]{0,1:T(8,128)(2,1)} copy(bf16[1024,2048]{1,0:T(8,128)(2,1)} %gather_fusion) | data formatting | bytes 8388608 | tf_op jit(solution)/shard_map/jit(_take)/gather | solution.py:44
  55.1 5.4 %fusion.3 = bf16[2048,1024]{1,0:T(8,128)(2,1)} fusion(f32[1024]{0:T(1024)S(1)} %bitcast.22, bf16[1024,2048]{0,1:T(8,128)(2,1)} %copy.14, pred[1024]{0:T(1024)(128)(4,1)S(1)} %compare_and_fusion.1), kind=kLoop, calls=%fused_computation.10 | loop fusion | flops 8388608 | bytes 8393728 | tf_op jit(solution)/shard_map/convert_element_type | solution.py:44
  60.4 3.9 collective-permute-start.1
  64.4 6.0 %broadcast_select_fusion.3 = (bf16[2048,1024]{1,0:T(8,128)(2,1)}, bf16[2048,1024]{1,0:T(8,128)(2,1)}) fusion(bf16[2048,1024]{1,0:T(8,128)(2,1)} %param.6, pred[]{:T(512)S(6)} %eq.16, pred[]{:T(512)S(6)} %eq.18), kind=kLoop, calls=%fused_computation.14 | loop fusion | flops 4194304 | bytes 12582914 | tf_op jit(solution)/shard_map/jit(_where)/select_n | solution.py:23
  72.3 251.8 %collective-permute-done.1 = bf16[2048,1024]{1,0:T(8,128)(2,1)} collective-permute-done((bf16[2048,1024]{1,0:T(8,128)(2,1)}, bf16[2048,1024]{1,0:T(8,128)(2,1)}, u32[]{:S(2)}, u32[]{:S(2)}) %collective-permute-start.1) | collective-permute-done | bytes 4194336 | tf_op jit(solution)/shard_map/ppermute | solution.py:18
  324.1 14.7 %add_convert_fusion = bf16[2048,1024]{1,0:T(8,128)(2,1)} fusion(bf16[2048,1024]{1,0:T(8,128)(2,1)} %collective-permute-done.1, bf16[2048,1024]{1,0:T(8,128)(2,1)} %param.6, bf16[2048,1024]{0,1:T(8,128)(2,1)} %get-tuple-element.9, bf16[2048,1024]{0,1:T(8,128)(2,1)} %get-tuple-element.8), kind=kOutput, calls=%fused_computation.9 | convolution fusion | flops 8613003264 | bytes 20971520 | tf_op jit(solution)/shard_map/dot_general | solution.py:47
  338.8 13.7 %gather_fusion.1 = bf16[2048,1024]{1,0:T(8,128)(2,1)} fusion(bf16[2048,1024]{1,0:T(8,128)(2,1)} %add_convert_fusion, s32[2048]{0:T(1024)S(1)} %broadcast_clamp_fusion), kind=kCustom, calls=%fused_computation.1 | custom fusion | bytes 8396800 | tf_op jit(solution)/shard_map/jit(_take)/gather | solution.py:53
  352.5 4.2 multiply_convert_fusion.1
  356.7 1.6 collective-permute-start.2
  358.3 44.8 %all-reduce.3.cloned.1.call-done = (bf16[2048,1024]{1,0:T(8,128)(2,1)}, bf16[2048,1024]{1,0:T(8,128)(2,1)}) async-done(((bf16[2048,1024]{1,0:T(8,128)(2,1)}, bf16[2048,1024]{1,0:T(8,128)(2,1)}), (bf16[2048,1024]{1,0:T(8,128)(2,1)}, bf16[2048,1024]{1,0:T(8,128)(2,1)})) %all-reduce.3.cloned.1.call-update) | async-done | bytes 8388624 | tf_op jit(solution)/shard_map/psum | solution.py:23
  403.2 7.9 %fusion.4 = f32[1024,1024]{1,0:T(8,128)S(1)} fusion(bf16[2048,1024]{1,0:T(8,128)(2,1)} %get-tuple-element.3, bf16[2048,1024]{1,0:T(8,128)(2,1)} %add_convert_fusion), kind=kOutput, calls=%fused_computation.27 | convolution fusion | flops 4294967296 | bytes 12582912 | tf_op jit(solution)/shard_map/dot_general | solution.py:61
  411.1 4.6 fusion.5
  415.8 33.4 %collective-permute-done.2 = bf16[2048,1024]{1,0:T(8,128)(2,1)} collective-permute-done((bf16[2048,1024]{1,0:T(8,128)(2,1)}, bf16[2048,1024]{1,0:T(8,128)(2,1)}, u32[]{:S(2)}, u32[]{:S(2)}) %collective-permute-start.2) | collective-permute-done | bytes 4194336 | tf_op jit(solution)/shard_map/ppermute | solution.py:18
  449.1 4.1 fusion.2
  453.3 2.0 copy-done.2
  455.3 2.6 fusion.6
  457.9 39.2 %reduce-scatter.2.cloned.1.call-done = f32[256,256]{1,0:T(8,128)} async-done(((f32[2048,256]{1,0:T(8,128)}), f32[256,256]{1,0:T(8,128)}) %reduce-scatter.2.cloned.1.call-update) | async-done | bytes 262160 | tf_op jit(solution)/shard_map/reduce_scatter | solution.py:71
  (20 shorter events, 2.4 us)
Async XLA Ops:
  7.2 448.1 %copy-start = (bf16[1024,256]{1,0:T(8,128)(2,1)S(1)}, bf16[1024,256]{1,0:T(8,128)(2,1)}, u32[]{:S(2)}) copy-start(bf16[1024,256]{1,0:T(8,128)(2,1)} %param.9) | copy-start | bytes 1572868
  7.2 396.0 %all-reduce.3.cloned.1.call-start = ((), (), s32[]{:S(2)}) async-start(), calls=%async_computation.2 | async-start | bytes 16777216 | tf_op jit(solution)/shard_map/psum | solution.py:23
  13.7 7.6 %collective-permute-start = (bf16[2048,1024]{0,1:T(8,128)(2,1)}, bf16[2048,1024]{0,1:T(8,128)(2,1)}, u32[]{:S(2)}, u32[]{:S(2)}) collective-permute-start(bf16[2048,1024]{0,1:T(8,128)(2,1)} %copy.12), channel_id=1, source_target_pairs={{0,1},{1,0},{2,3},{3,2},{4,5},{5,4},{6,7},{7,6},{8,9},{9,8},{10,11... | collective-permute-start | bytes 12582920 | tf_op jit(solution)/shard_map/ppermute | solution.py:12
  60.4 263.7 %collective-permute-start.1 = (bf16[2048,1024]{1,0:T(8,128)(2,1)}, bf16[2048,1024]{1,0:T(8,128)(2,1)}, u32[]{:S(2)}, u32[]{:S(2)}) collective-permute-start(bf16[2048,1024]{1,0:T(8,128)(2,1)} %fusion.3), channel_id=1, source_target_pairs={{0,4},{1,5},{2,6},{3,7},{4,0},{5,1},{6,2},{7,3},{8,12},{9,13},{10,... | collective-permute-start | bytes 12582920 | tf_op jit(solution)/shard_map/ppermute | solution.py:18
  70.5 426.6 %reduce-scatter.2.cloned.1.call-start = ((), (), s32[]{:S(2)}) async-start(), calls=%async_computation.1 | async-start | bytes 2359296 | tf_op jit(solution)/shard_map/reduce_scatter | solution.py:71
  356.7 92.5 %collective-permute-start.2 = (bf16[2048,1024]{1,0:T(8,128)(2,1)}, bf16[2048,1024]{1,0:T(8,128)(2,1)}, u32[]{:S(2)}, u32[]{:S(2)}) collective-permute-start(bf16[2048,1024]{1,0:T(8,128)(2,1)} %multiply_convert_fusion.1), channel_id=1, source_target_pairs={{0,16},{8,24},{16,0},{24,8},{1,17},{9,25},{17,1},{25,9},{2,18},{10... | collective-permute-start | bytes 12582920 | tf_op jit(solution)/shard_map/ppermute | solution.py:18
  403.1 8.0 %copy-start.1 = (bf16[2048,1024]{1,0:T(8,128)(2,1)S(1)}, bf16[2048,1024]{1,0:T(8,128)(2,1)}, u32[]{:S(2)}) copy-start(bf16[2048,1024]{1,0:T(8,128)(2,1)} %add_convert_fusion) | copy-start | bytes 12582916
  403.1 8.0 %copy-start.3 = (bf16[2048,1024]{1,0:T(8,128)(2,1)S(1)}, bf16[2048,1024]{1,0:T(8,128)(2,1)}, u32[]{:S(2)}) copy-start(bf16[2048,1024]{1,0:T(8,128)(2,1)} %get-tuple-element.2) | copy-start | bytes 12582916
  453.3 2.0 copy-start.2
Sparse Core Ops, SparseCore 0:
  70.6 332.5 all-reduce.2
  458.0 38.9 reduce-scatter.1
where the time goes:
time: 505 us; the launch traced here: 504 us
  waiting for transfers between devices  375 us (74%)
  local copies, waits for them, and re-layouts  43.5 us (9%)
  other arithmetic  35.4 us (7%)
  matrix products  29.8 us (6%)
  between operations  14.1 us (3%)
  starting transfers between devices  6.31 us (1%)
    ppermute x2, waiting for transfers between devices, shifted(): return lax.ppermute(value, axis, pairs)  285 us
    psum x1, waiting for transfers between devices, spread(): return lax.psum(jnp.where(mine, x, jnp.zeros_like(x)), axis)  44.8 us
    reduce_scatter x1, waiting for transfers between devices, on_device(): lax.psum_scatter(partial_value, 'col', scatter_dimension=0, tiled=True)  39.2 us
    gather x2, local copies, waits for them, and re-layouts, on_device(): jnp.take(whole_block, own_perm, axis=1) * own_scale[None, :]  19.7 us
    dot_general x1, matrix products, on_device(): jnp.dot(whole_block, diag_blocks, preferred_element_type=jnp.float32)  14.7 us
    gather x1, local copies, waits for them, and re-layouts, on_device(): jnp.take(mixed, perm_rows, axis=0) * scale_rows[:, None]  13.7 us
    dot_general x2, matrix products, on_device(): lax.dot_general(left_half, mixed, (((0,), (0,)), ((), ())), preferred_ele...  12.6 us
  transfers between devices with their start and end apart: 5, of which 5 were waited for; matrix products, arithmetic and copies ran while one was open for 11% of the time, Pallas kernels for 0%

commit v1 on v0

--- a/solution.py
+++ b/solution.py
@@ -20,7 +20,7 @@
 
 def spread(x, axis, root):
     mine = lax.axis_index(axis) == root
-    return lax.psum(jnp.where(mine, x, jnp.zeros_like(x)), axis)
+    return jnp.sum(lax.all_gather(jnp.where(mine, x, jnp.zeros_like(x)), axis), axis=0)
 
 
 def on_device(sim, diag_blocks, match_perm, match_scale, features):

time: 505 us -> 850 us (1.68)
  waiting for transfers between devices: 375 us -> 684 us
  other arithmetic: 35.4 us -> 70.7 us
    all_gather x0 -> x2, waiting for transfers between devices: none -> 261 us  [spread(): lax.all_gather(jnp.where(mine, x, jnp.zeros_like(x)), axis)]
    ppermute x2, waiting for transfers between devices: 285 us -> 382 us  [shifted(): return lax.ppermute(value, axis, pairs)]
    psum x1 -> x0, waiting for transfers between devices: 44.8 us -> none  [spread(): return lax.psum(jnp.where(mine, x, jnp.zeros_like(x)), axis)]
    reduce_sum x0 -> x2, other arithmetic: none -> 32.4 us  [spread(): jnp.sum(lax.all_gather(jnp.where(mine, x, jnp.zeros_like(x)), axis), axis=0)]
  transfers between devices with their start and end apart: 5 -> 6, of which waited for: 5 -> 4; matrix products, arithmetic and copies ran while one was open for 11% -> 15% of each run, Pallas kernels for 0% -> 0%
where the time goes in v1:
time: 850 us
  waiting for transfers between devices  684 us (80%)
  other arithmetic  70.7 us (8%)
  local copies, waits for them, and re-layouts  43.6 us (5%)
  matrix products  30 us (4%)
  between operations  13.9 us (2%)
    ppermute x2, waiting for transfers between devices, shifted(): return lax.ppermute(value, axis, pairs)  382 us
    all_gather x2, waiting for transfers between devices, spread(): lax.all_gather(jnp.where(mine, x, jnp.zeros_like(x)), axis)  261 us
    reduce_scatter x1, waiting for transfers between devices, on_device(): lax.psum_scatter(partial_value, 'col', scatter_dimension=0, tiled=True)  34.4 us
    reduce_sum x2, other arithmetic, spread(): jnp.sum(lax.all_gather(jnp.where(mine, x, jnp.zeros_like(x)), axis), axis=0)  32.4 us
    gather x2, local copies, waits for them, and re-layouts, on_device(): jnp.take(whole_block, own_perm, axis=1) * own_scale[None, :]  19.8 us
  transfers between devices with their start and end apart: 6, of which 4 were waited for; matrix products, arithmetic and copies ran while one was open for 15% of the time, Pallas kernels for 0%

profile of v1, /device:TPU:0, one launch (start us, length us, event | category | flops | bytes accessed | tf_op | source)
XLA Modules:
  0.0 849.6 jit_solution(15762607525282985172)
XLA Ops:
  7.2 6.2 broadcast_select_fusion.3
  14.2 6.5 copy.12
  22.0 0.8 compare_select_fusion.1
  22.9 5.5 collective-permute-done
  28.4 8.2 broadcast_select_fusion.2
  36.6 8.3 pad_maximum_fusion
  44.9 13.3 %gather_fusion = bf16[1024,2048]{1,0:T(8,128)(2,1)} fusion(bf16[2048,2048]{0,1:T(8,128)(2,1)} %pad_maximum_fusion, s32[1024]{0:T(1024)S(1)} %broadcast_clamp_fusion.1), kind=kCustom, calls=%fused_computation | custom fusion | bytes 8392704 | tf_op jit(solution)/shard_map/jit(_take)/gather | solution.py:44
  58.3 6.4 copy.14
  64.7 5.6 fusion.3
  70.3 5.4 collective-permute-start.1
  77.3 382.2 %collective-permute-done.1 = bf16[2048,1024]{1,0:T(8,128)(2,1)} collective-permute-done((bf16[2048,1024]{1,0:T(8,128)(2,1)}, bf16[2048,1024]{1,0:T(8,128)(2,1)}, u32[]{:S(2)}, u32[]{:S(2)}) %collective-permute-start.1) | collective-permute-done | bytes 4194336 | tf_op jit(solution)/shard_map/ppermute | solution.py:18
  459.4 15.0 %add_convert_fusion = bf16[2048,1024]{1,0:T(8,128)(2,1)} fusion(bf16[2048,1024]{1,0:T(8,128)(2,1)} %collective-permute-done.1, bf16[2048,1024]{1,0:T(8,128)(2,1)} %param.6, bf16[2048,1024]{0,1:T(8,128)(2,1)} %get-tuple-element.7, bf16[2048,1024]{0,1:T(8,128)(2,1)} %get-tuple-element.6), kind=kOutput, calls=%fused_computation.9 | convolution fusion | flops 8613003264 | bytes 20971520 | tf_op jit(solution)/shard_map/dot_general | solution.py:47
  474.4 13.7 %gather_fusion.1 = bf16[2048,1024]{1,0:T(8,128)(2,1)} fusion(bf16[2048,1024]{1,0:T(8,128)(2,1)} %add_convert_fusion, s32[2048]{0:T(1024)S(1)} %broadcast_clamp_fusion), kind=kCustom, calls=%fused_computation.1 | custom fusion | bytes 8396800 | tf_op jit(solution)/shard_map/jit(_take)/gather | solution.py:53
  488.2 4.3 multiply_convert_fusion.1
  492.5 1.6 collective-permute-start.2
  494.1 18.2 %reduce_sum.25 = bf16[2048,1024]{1,0:T(8,128)(2,1)} reduce(bf16[8,2048,1024]{2,1,0:T(8,128)(2,1)} %bitcast.21, bf16[]{:T(256)} %constant.100.clone.1), dimensions={0}, to_apply=%region_1.2 | reduce | flops 14680064 | bytes 37748736 | tf_op jit(solution)/shard_map/reduce_sum | solution.py:23
  512.2 261.1 %all-gather.5.cloned.1.call-done = bf16[16384,1024]{1,0:T(8,128)(2,1)} async-done(((bf16[2048,1024]{1,0:T(8,128)(2,1)}), bf16[16384,1024]{1,0:T(8,128)(2,1)}) %all-gather.5.cloned.1.call-update) | async-done | bytes 33554448 | tf_op jit(solution)/shard_map/all_gather | solution.py:23
  773.3 14.2 %reduce_sum.24 = bf16[2048,1024]{1,0:T(8,128)(2,1)} reduce(bf16[8,2048,1024]{2,1,0:T(8,128)(2,1)} %bitcast.22, bf16[]{:T(256)} %constant.100.clone.1), dimensions={0}, to_apply=%region_0.1 | reduce | flops 14680064 | bytes 37748736 | tf_op jit(solution)/shard_map/reduce_sum | solution.py:23
  787.5 7.7 fusion.5
  795.3 4.6 fusion.4
  799.9 4.1 fusion.2
  804.0 2.0 copy-done.3
  806.1 2.6 fusion.6
  808.7 34.4 %reduce-scatter.2.cloned.1.call-done = f32[256,256]{1,0:T(8,128)} async-done(((f32[2048,256]{1,0:T(8,128)}), f32[256,256]{1,0:T(8,128)}) %reduce-scatter.2.cloned.1.call-update) | async-done | bytes 262160 | tf_op jit(solution)/shard_map/reduce_scatter | solution.py:71
  (25 shorter events, 3.7 us)
Async XLA Ops:
  7.2 798.9 %copy-start = (bf16[1024,256]{1,0:T(8,128)(2,1)S(1)}, bf16[1024,256]{1,0:T(8,128)(2,1)}, u32[]{:S(2)}) copy-start(bf16[1024,256]{1,0:T(8,128)(2,1)} %param.9) | copy-start | bytes 1572868
  7.2 486.9 %all-gather.7.cloned.1.call-start = ((), (), s32[]{:S(2)}) async-start(), calls=%async_computation.3 | async-start | bytes 37748736 | tf_op jit(solution)/shard_map/all_gather | solution.py:23
  13.4 759.9 %all-gather.5.cloned.1.call-start = ((), (), s32[]{:S(2)}) async-start(), calls=%async_computation.2 | async-start | bytes 37748736 | tf_op jit(solution)/shard_map/all_gather | solution.py:23
  14.2 828.9 %reduce-scatter.2.cloned.1.call-start = ((), (), s32[]{:S(2)}) async-start(), calls=%async_computation.1 | async-start | bytes 2359296 | tf_op jit(solution)/shard_map/reduce_scatter | solution.py:71
  20.7 7.6 collective-permute-start
  70.3 389.2 %collective-permute-start.1 = (bf16[2048,1024]{1,0:T(8,128)(2,1)}, bf16[2048,1024]{1,0:T(8,128)(2,1)}, u32[]{:S(2)}, u32[]{:S(2)}) collective-permute-start(bf16[2048,1024]{1,0:T(8,128)(2,1)} %fusion.3), channel_id=1, source_target_pairs={{0,4},{1,5},{2,6},{3,7},{4,0},{5,1},{6,2},{7,3},{8,12},{9,13},{10,... | collective-permute-start | bytes 12582920 | tf_op jit(solution)/shard_map/ppermute | solution.py:18
  492.5 307.5 %collective-permute-start.2 = (bf16[2048,1024]{1,0:T(8,128)(2,1)}, bf16[2048,1024]{1,0:T(8,128)(2,1)}, u32[]{:S(2)}, u32[]{:S(2)}) collective-permute-start(bf16[2048,1024]{1,0:T(8,128)(2,1)} %multiply_convert_fusion.1), channel_id=1, source_target_pairs={{0,16},{8,24},{16,0},{24,8},{1,17},{9,25},{17,1},{25,9},{2,18},{10... | collective-permute-start | bytes 12582920 | tf_op jit(solution)/shard_map/ppermute | solution.py:18
  787.5 7.7 copy-start.1
  787.5 7.7 copy-start.2
  804.0 2.0 copy-start.3
Sparse Core Ops, SparseCore 0:
  13.5 470.7 all-gather.6
  486.5 286.7 all-gather.4
  808.8 34.2 reduce-scatter.1
